TPU v7x, 32 devices: a whole 2x2x4 slice. The times are simulated.
32 devices in a mesh: vocab: 8 (over y, x, core), blk: 4 (over z).
Axes of the slice: x: 2, y: 2, z: 4, core: 2. Of those that a mesh axis runs over, the one named last changes fastest.
Arguments:
- char_ids: int32 [16384, 50], P(('vocab', 'blk')), may hold values from 0 to 255, as said below
- char_table: bfloat16 [256, 16], replicated, may hold values from -5 to 5
- conv_weight: bfloat16 [112, 896], replicated, may hold values from -0.75 to 0.75
- proj_weight: bfloat16 [896, 1024], replicated, may hold values from -0.1875 to 0.1875
- gate_weight: bfloat16 [2, 1024, 1024], replicated, may hold values from -0.1875 to 0.1875
- trans_weight: bfloat16 [2, 1024, 1024], replicated, may hold values from -0.1875 to 0.1875
- gate_bias: float32 [2, 1024], replicated, may hold values from -4 to 4
- hidden: bfloat16 [2048, 1024], P(('vocab', 'blk')), may hold values from -48 to 48
- targets: int32 [2048], P(('vocab', 'blk')), may hold values from 0 to 16383
Outputs:
- row_loss: float32 [2048], P(('vocab', 'blk'))
- hidden_grad: bfloat16 [2048, 1024], P(('vocab', 'blk'))
Inputs may be any that keep to these rules, and one draw needn't show every extreme that they name: `char_ids`: each word has 2 to 50 characters with ids 1 and up, followed by the padding id 0.
All inputs are finite; a program needn't handle non-finite values.
Results may differ from a plain program's by a relative error of at most 0.014.
The roundings to bfloat16 on the way count: a program that leaves them out, or rounds other values in their place, can miss the bound.
Values may be sent and summed in bfloat16 or wider, within the bound.
No kernel may reach another device: no remote copies, remote signals or barrier semaphores. Data moves between devices by JAX's collectives and lax.ppermute only.
A program may use at most 128 MiB of HBM per device.

v0:
```python
import math
import jax
import jax.numpy as jnp
from jax import lax
from jax.sharding import PartitionSpec as P


def shifted(array, axis, by):
    count = lax.axis_size(axis)
    return lax.ppermute(array, axis, [(i, (i + by) % count) for i in range(count)])


def char_features(char_ids, char_table, conv_weight):
    num_words = char_ids.shape[0]
    length = char_ids.shape[1]
    symbols = char_table.shape[0]
    embed_dim = char_table.shape[1]
    widths = conv_weight.shape[0] // embed_dim
    filters = conv_weight.shape[1] // widths
    onehot = (char_ids[:, :, None] == jnp.arange(symbols, dtype=jnp.int32)[None, None, :]).astype(
        jnp.bfloat16
    )
    vectors = jnp.dot(
        onehot.reshape(num_words * length, symbols), char_table, preferred_element_type=jnp.float32
    )
    vectors = vectors.astype(jnp.bfloat16).reshape(num_words, length, embed_dim)
    padded = jnp.pad(vectors, ((0, 0), (0, widths - 1), (0, 0)))
    windows = jnp.concatenate(
        [padded[:, shift_at : shift_at + length, :] for shift_at in range(widths)], axis=2
    )
    offset = jnp.arange(widths * embed_dim) // embed_dim
    kernel = jnp.arange(widths * filters) // filters + 1
    masked = jnp.where(offset[:, None] < kernel[None, :], conv_weight, jnp.zeros_like(conv_weight))
    conv_out = jnp.dot(
        windows.reshape(num_words * length, widths * embed_dim),
        masked,
        preferred_element_type=jnp.float32,
    )
    conv_out = conv_out.reshape(num_words, length, widths * filters)
    position = jnp.arange(length)
    usable = position[:, None] <= length - kernel[None, :]
    pooled = jnp.max(jnp.where(usable[None, :, :], conv_out, -jnp.inf), axis=1)
    return jnp.tanh(pooled).astype(jnp.bfloat16)


def embed_words(
    char_ids, char_table, conv_weight, proj_weight, gate_weight, trans_weight, gate_bias
):
    features = char_features(char_ids, char_table, conv_weight)
    current = jnp.dot(features, proj_weight, preferred_element_type=jnp.float32).astype(
        jnp.bfloat16
    )
    for layer_idx in range(gate_weight.shape[0]):
        opened = jax.nn.sigmoid(
            jnp.dot(current, gate_weight[layer_idx], preferred_element_type=jnp.float32)
            + gate_bias[layer_idx]
        )
        carried = jax.nn.relu(
            jnp.dot(current, trans_weight[layer_idx], preferred_element_type=jnp.float32)
        )
        current = (opened * carried + (1.0 - opened) * current.astype(jnp.float32)).astype(
            jnp.bfloat16
        )
    return current


def embed_all(char_ids, char_table, conv_weight, proj_weight, gate_weight, trans_weight, gate_bias):
    num_total = char_ids.shape[0]
    block_size = math.gcd(num_total, 128)
    grouped = char_ids.reshape(num_total // block_size, block_size, char_ids.shape[1])

    def one_block(piece_ids):
        return embed_words(
            piece_ids, char_table, conv_weight, proj_weight, gate_weight, trans_weight, gate_bias
        )

    return lax.map(one_block, grouped).reshape(num_total, proj_weight.shape[1])


def pick_targets(word_panel, row_spot):
    count_words = word_panel.shape[0]
    inside = (row_spot >= 0) & (row_spot < count_words)
    picked = jnp.take(word_panel, jnp.clip(row_spot, 0, count_words - 1), axis=0).astype(
        jnp.float32
    )
    return jnp.where(inside[:, None], picked, jnp.zeros_like(picked))


def fold_panel(acc_state, row_block, row_spot, word_panel):
    run_max, run_total, weighted, target_vec = acc_state
    scores = lax.dot_general(
        row_block, word_panel, (((1,), (1,)), ((), ())), preferred_element_type=jnp.float32
    )
    new_max = jnp.maximum(run_max, jnp.max(scores, axis=1))
    rescale = jnp.exp(run_max - new_max)
    soft_weights = jnp.exp(scores - new_max[:, None]).astype(jnp.bfloat16)
    run_total = run_total * rescale + jnp.sum(soft_weights.astype(jnp.float32), axis=1)
    weighted = weighted * rescale[:, None] + jnp.dot(
        soft_weights, word_panel, preferred_element_type=jnp.float32
    )
    target_vec = target_vec + pick_targets(word_panel, row_spot)
    return (new_max, run_total, weighted, target_vec)


def finish_rows(hidden, run_max, run_total, weighted, target_vec):
    target_score = jnp.sum(hidden.astype(jnp.float32) * target_vec, axis=1)
    row_loss = run_max + jnp.log(run_total) - target_score
    hidden_grad = (weighted / run_total[:, None] - target_vec).astype(jnp.bfloat16)
    return (row_loss, hidden_grad)


def per_device(
    char_ids,
    char_table,
    conv_weight,
    proj_weight,
    gate_weight,
    trans_weight,
    gate_bias,
    hidden,
    targets,
):
    embeds = embed_all(
        char_ids, char_table, conv_weight, proj_weight, gate_weight, trans_weight, gate_bias
    )
    local_words = embeds.shape[0]
    my_rows = hidden.shape[0]
    model_dim = hidden.shape[1]
    blocks = lax.axis_size("blk")
    group_idx = lax.axis_index("blk")
    word_panel = lax.all_gather(embeds, "vocab", axis=0, tiled=True)
    group_hidden = lax.all_gather(hidden, "blk", axis=0, tiled=True)
    group_goal = lax.all_gather(targets, "blk", axis=0, tiled=True)
    owner_dev = group_goal // local_words
    in_group = owner_dev % blocks == group_idx
    spot_all = jnp.where(in_group, owner_dev // blocks * local_words + group_goal % local_words, -1)
    running = (
        jnp.full((my_rows,), -jnp.inf, jnp.float32),
        jnp.zeros((my_rows,), jnp.float32),
        jnp.zeros((my_rows, model_dim), jnp.float32),
        jnp.zeros((my_rows, model_dim), jnp.float32),
    )
    for step_idx in range(blocks):
        which_block = (group_idx - step_idx) % blocks
        row_block = lax.dynamic_slice_in_dim(group_hidden, which_block * my_rows, my_rows, 0)
        row_spot = lax.dynamic_slice_in_dim(spot_all, which_block * my_rows, my_rows, 0)
        running = fold_panel(running, row_block, row_spot, word_panel)
        running = shifted((running[0], running[1], running[2], running[3]), "blk", 1)
    run_max, run_total, weighted, target_vec = running
    return finish_rows(hidden, run_max, run_total, weighted, target_vec)


def solution(mesh):
    return jax.shard_map(
        per_device,
        mesh=mesh,
        in_specs=(
            P(("vocab", "blk"), None),
            P(),
            P(),
            P(),
            P(),
            P(),
            P(),
            P(("vocab", "blk"), None),
            P(("vocab", "blk")),
        ),
        out_specs=(P(("vocab", "blk")), P(("vocab", "blk"), None)),
        check_vma=False,
    )
```

profile of v0, /device:TPU:0, one launch (start us, length us, event | category | flops | bytes accessed | tf_op | source)
XLA Modules:
  0.0 273.5 jit_solution(3712595097836582395)
XLA Ops:
  8.3 100.8 %while.13 = (s32[]{:T(128)}, bf16[4,128,1024]{2,1,0:T(8,128)(2,1)}, s32[4,128,50]{2,1,0:T(8,128)S(1)}, bf16[256,16]{0,1:T(8,128)(2,1)}, bf16[112,896]{1,0:T(8,12...) while((s32[]{:T(128)}, bf16[4,128,1024]{2,1,0:T(8,128)(2,1)}, ...), condition=%wide.region_2.3_spmd, body=%wide.region_0.2_spmd.sunk | while | flops 2662044928 | bytes 67010176 | solution.py:77
  8.5 4.2 %convolution_convert_fusion.4 = bf16[6400,16]{0,1:T(8,128)(2,1)S(1)} fusion(bf16[256,16]{0,1:T(8,128)(2,1)} %get-tuple-element.308, s32[6400]{0:T(1024)S(1)} %eq.53), kind=kOutput, calls=%fused_computation.5.clone.1 | convolution fusion | flops 54169600 | bytes 238592 | tf_op jit(solution)/shard_map/while/body/eval_jaxpr/dot_general | solution.py:23
  24.2 4.8 %select_reduce_fusion.2 = f32[128,896]{1,0:T(8,128)S(1)} fusion(pred[50,896]{1,0:T(8,128)(4,1)S(1)} %iota_compare_fusion.6, bf16[128,50,112]{0,2,1:T(8,128)(2,1)} %constant_dynamic-update-slice_fusion.20, bf16[112,896]{1,0:T(8,128)(2,1)S(1)} %copy-done.9, s32[896]{0:T(1024)S(1)} %fusion.150, s32[112]{0:T(128)S(1)} %and_select_fusion.6), kind=kOutput, calls=%fused_computation.4.clone.1 | convolution fusion | flops 1296060416 | bytes 2141888 | tf_op jit(solution)/shard_map/while/body/eval_jaxpr/dot_general | solution.py:34
  33.7 4.2 %convolution_convert_fusion.4 = bf16[6400,16]{0,1:T(8,128)(2,1)S(1)} fusion(bf16[256,16]{0,1:T(8,128)(2,1)} %get-tuple-element.308, s32[6400]{0:T(1024)S(1)} %eq.53), kind=kOutput, calls=%fused_computation.5.clone.1 | convolution fusion | flops 54169600 | bytes 238592 | tf_op jit(solution)/shard_map/while/body/eval_jaxpr/dot_general | solution.py:23
  49.4 4.8 %select_reduce_fusion.2 = f32[128,896]{1,0:T(8,128)S(1)} fusion(pred[50,896]{1,0:T(8,128)(4,1)S(1)} %iota_compare_fusion.6, bf16[128,50,112]{0,2,1:T(8,128)(2,1)} %constant_dynamic-update-slice_fusion.20, bf16[112,896]{1,0:T(8,128)(2,1)S(1)} %copy-done.9, s32[896]{0:T(1024)S(1)} %fusion.150, s32[112]{0:T(128)S(1)} %and_select_fusion.6), kind=kOutput, calls=%fused_computation.4.clone.1 | convolution fusion | flops 1296060416 | bytes 2141888 | tf_op jit(solution)/shard_map/while/body/eval_jaxpr/dot_general | solution.py:34
  58.9 4.2 %convolution_convert_fusion.4 = bf16[6400,16]{0,1:T(8,128)(2,1)S(1)} fusion(bf16[256,16]{0,1:T(8,128)(2,1)} %get-tuple-element.308, s32[6400]{0:T(1024)S(1)} %eq.53), kind=kOutput, calls=%fused_computation.5.clone.1 | convolution fusion | flops 54169600 | bytes 238592 | tf_op jit(solution)/shard_map/while/body/eval_jaxpr/dot_general | solution.py:23
  74.6 4.8 %select_reduce_fusion.2 = f32[128,896]{1,0:T(8,128)S(1)} fusion(pred[50,896]{1,0:T(8,128)(4,1)S(1)} %iota_compare_fusion.6, bf16[128,50,112]{0,2,1:T(8,128)(2,1)} %constant_dynamic-update-slice_fusion.20, bf16[112,896]{1,0:T(8,128)(2,1)S(1)} %copy-done.9, s32[896]{0:T(1024)S(1)} %fusion.150, s32[112]{0:T(128)S(1)} %and_select_fusion.6), kind=kOutput, calls=%fused_computation.4.clone.1 | convolution fusion | flops 1296060416 | bytes 2141888 | tf_op jit(solution)/shard_map/while/body/eval_jaxpr/dot_general | solution.py:34
  84.1 4.2 %convolution_convert_fusion.4 = bf16[6400,16]{0,1:T(8,128)(2,1)S(1)} fusion(bf16[256,16]{0,1:T(8,128)(2,1)} %get-tuple-element.308, s32[6400]{0:T(1024)S(1)} %eq.53), kind=kOutput, calls=%fused_computation.5.clone.1 | convolution fusion | flops 54169600 | bytes 238592 | tf_op jit(solution)/shard_map/while/body/eval_jaxpr/dot_general | solution.py:23
  99.8 4.8 %select_reduce_fusion.2 = f32[128,896]{1,0:T(8,128)S(1)} fusion(pred[50,896]{1,0:T(8,128)(4,1)S(1)} %iota_compare_fusion.6, bf16[128,50,112]{0,2,1:T(8,128)(2,1)} %constant_dynamic-update-slice_fusion.20, bf16[112,896]{1,0:T(8,128)(2,1)S(1)} %copy-done.9, s32[896]{0:T(1024)S(1)} %fusion.150, s32[112]{0:T(128)S(1)} %and_select_fusion.6), kind=kOutput, calls=%fused_computation.4.clone.1 | convolution fusion | flops 1296060416 | bytes 2141888 | tf_op jit(solution)/shard_map/while/body/eval_jaxpr/dot_general | solution.py:34
  110.7 9.9 %all-reduce.1 = s32[256]{0:T(256)S(1)} all-reduce(s32[256]{0:T(256)S(1)} %dynamic-update-slice), channel_id=1, replica_groups=mesh['vocab'=8,'blk'=4] {'blk'}, use_global_device_ids=true, to_apply=%add.1 | all-reduce | flops 256 | bytes 2048
  121.3 15.9 %all_gather.9 = bf16[256,1024]{1,0:T(8,128)(2,1)S(1)} all-gather(bf16[64,1024]{1,0:T(8,128)(2,1)} %param.20), channel_id=1, replica_groups=mesh['vocab'=8,'blk'=4] {'blk'}, dimensions={0}, use_global_device_ids=true | all-gather | bytes 655360 | tf_op jit(solution)/shard_map/all_gather | solution.py:132
  137.3 29.1 %all-gather.2.cloned.1.call-done = bf16[4096,1024]{1,0:T(8,128)(2,1)} async-done(((bf16[512,1024]{1,0:T(8,128)(2,1)}), bf16[4096,1024]{1,0:T(8,128)(2,1)}) %all-gather.2.cloned.1.call-update) | async-done | bytes 8388624 | tf_op jit(solution)/shard_map/all_gather | solution.py:131
  166.3 5.3 %gather_fusion = bf16[64,1024]{1,0:T(8,128)(2,1)S(1)} fusion(bf16[4096,1024]{1,0:T(8,128)(2,1)} %all-gather.2.cloned.1.call-done, s32[1024]{0:T(1024)S(1)} %pad_clamp_fusion.3), kind=kCustom, calls=%fused_computation.clone | custom fusion | bytes 262400 | tf_op jit(solution)/shard_map/jit(_take)/gather | solution.py:83
  173.9 6.7 %fusion.101 = (f32[64]{0:T(128)S(1)}, f32[64,4096]{1,0:T(8,128)S(1)}) fusion(bf16[4096,1024]{1,0:T(8,128)(2,1)} %all-gather.2.cloned.1.call-done, bf16[256,1024]{1,0:T(8,128)(2,1)S(1)} %all_gather.9, s32[]{:T(128)S(6)} %select_n.128), kind=kOutput, calls=%fused_computation.147 | convolution fusion | flops 537132992 | bytes 9568516 | tf_op jit(solution)/shard_map/dot_general | solution.py:91
  187.1 3.3 %fusion.102 = (f32[64]{0:T(128)}, f32[64,4096]{1,0:T(8,128)S(1)}) fusion(bf16[4096,1024]{1,0:T(8,128)(2,1)S(1)} %copy-done, bf16[256,1024]{1,0:T(8,128)(2,1)S(1)} %all_gather.9, s32[]{:T(128)S(6)} %select_n.130), kind=kOutput, calls=%fused_computation.148 | convolution fusion | flops 537132992 | bytes 9568516 | tf_op jit(solution)/shard_map/dot_general | solution.py:91
  193.6 4.2 %fusion.104 = (f32[64]{0:T(128)}, f32[64,4096]{1,0:T(8,128)S(1)}) fusion(bf16[4096,1024]{1,0:T(8,128)(2,1)S(1)} %copy-done, bf16[256,1024]{1,0:T(8,128)(2,1)} %copy-done.2, s32[]{:T(128)S(6)} %select_n.134), kind=kOutput, calls=%fused_computation.150 | convolution fusion | flops 537132992 | bytes 9568516 | tf_op jit(solution)/shard_map/dot_general | solution.py:91
  197.8 5.3 %gather_fusion.1 = bf16[64,1024]{1,0:T(8,128)(2,1)S(1)} fusion(bf16[4096,1024]{1,0:T(8,128)(2,1)} %all-gather.2.cloned.1.call-done, s32[1024]{0:T(1024)S(1)} %pad_clamp_fusion.2), kind=kCustom, calls=%fused_computation.1.clone | custom fusion | bytes 262400 | tf_op jit(solution)/shard_map/jit(_take)/gather | solution.py:83
  203.0 5.3 %gather_fusion.2 = bf16[64,1024]{1,0:T(8,128)(2,1)S(1)} fusion(bf16[4096,1024]{1,0:T(8,128)(2,1)} %all-gather.2.cloned.1.call-done, s32[1024]{0:T(1024)S(1)} %pad_clamp_fusion.1), kind=kCustom, calls=%fused_computation.2.clone | custom fusion | bytes 262400 | tf_op jit(solution)/shard_map/jit(_take)/gather | solution.py:83
  208.3 5.3 %gather_fusion.3 = bf16[64,1024]{1,0:T(8,128)(2,1)S(1)} fusion(bf16[4096,1024]{1,0:T(8,128)(2,1)} %all-gather.2.cloned.1.call-done, s32[1024]{0:T(1024)S(1)} %pad_clamp_fusion), kind=kCustom, calls=%fused_computation.3.clone | custom fusion | bytes 262400 | tf_op jit(solution)/shard_map/jit(_take)/gather | solution.py:83
  227.5 5.2 %multiply_add_fusion.2 = f32[64,1024]{1,0:T(8,128)S(1)} fusion(f32[64,1024]{1,0:T(8,128)} %collective-permute-done.12, f32[64]{0:T(128)S(1)} %get-tuple-element.173, bf16[4096,1024]{1,0:T(8,128)(2,1)} %all-gather.2.cloned.1.call-done, f32[64,4096]{1,0:T(8,128)S(1)} %get-tuple-element.209, f32[64]{0:T(128)S(1)} %max.43), kind=kOutput, calls=%fused_computation.88 | convolution fusion | flops 537526272 | bytes 9961984 | tf_op jit(solution)/shard_map/dot_general | solution.py:98
  233.0 4.1 %collective-permute-done.9 = f32[64,1024]{1,0:T(8,128)S(1)} collective-permute-done((f32[64,1024]{1,0:T(8,128)S(1)}, f32[64,1024]{1,0:T(8,128)S(1)}, u32[]{:S(2)}, u32[]{:S(2)}) %collective-permute-start.9) | collective-permute-done | bytes 262176 | tf_op jit(solution)/shard_map/ppermute | solution.py:10
  237.3 6.5 %collective-permute-done.13 = f32[64,1024]{1,0:T(8,128)S(1)} collective-permute-done((f32[64,1024]{1,0:T(8,128)S(1)}, f32[64,1024]{1,0:T(8,128)S(1)}, u32[]{:S(2)}, u32[]{:S(2)}) %collective-permute-start.13) | collective-permute-done | bytes 262176 | tf_op jit(solution)/shard_map/ppermute | solution.py:10
  248.8 6.4 %collective-permute-done.14 = f32[64,1024]{1,0:T(8,128)S(1)} collective-permute-done((f32[64,1024]{1,0:T(8,128)S(1)}, f32[64,1024]{1,0:T(8,128)S(1)}, u32[]{:S(2)}, u32[]{:S(2)}) %collective-permute-start.14) | collective-permute-done | bytes 262176 | tf_op jit(solution)/shard_map/ppermute | solution.py:10
  259.7 5.6 %collective-permute-done.7 = f32[64]{0:T(128)S(1)} collective-permute-done((f32[64]{0:T(128)S(1)}, f32[64]{0:T(128)S(1)}, u32[]{:S(2)}, u32[]{:S(2)}) %collective-permute-start.7) | collective-permute-done | bytes 288 | tf_op jit(solution)/shard_map/ppermute | solution.py:10
  (233 shorter events, 104.1 us)
Async XLA Ops:
  7.2 159.2 %all-gather.2.cloned.1.call-start = ((), (), s32[]{:S(2)}) async-start(), calls=%async_computation | async-start | bytes 9437184 | tf_op jit(solution)/shard_map/all_gather | solution.py:131
  8.2 100.9 %copy-start.11 = (u32[32]{0:T(128)S(1)}, u32[32]{0:T(128)}, u32[]{:S(2)}) copy-start(u32[32]{0:T(128)} %constant.224) | copy-start | bytes 388
  8.3 102.2 %copy-start.10 = (s32[64]{0:T(128)S(1)}, s32[64]{0:T(128)}, u32[]{:S(2)}) copy-start(s32[64]{0:T(128)} %param.21) | copy-start | bytes 772
  137.3 53.1 %copy-start.2 = (bf16[256,1024]{1,0:T(8,128)(2,1)}, bf16[256,1024]{1,0:T(8,128)(2,1)S(1)}, u32[]{:S(2)}) copy-start(bf16[256,1024]{1,0:T(8,128)(2,1)S(1)} %all_gather.9) | copy-start | bytes 1572868
  172.4 10.7 %copy-start = (bf16[4096,1024]{1,0:T(8,128)(2,1)S(1)}, bf16[4096,1024]{1,0:T(8,128)(2,1)}, u32[]{:S(2)}) copy-start(bf16[4096,1024]{1,0:T(8,128)(2,1)} %all-gather.2.cloned.1.call-done) | copy-start | bytes 25165828
  172.4 53.7 %collective-permute-start.8 = (f32[64,1024]{1,0:T(8,128)}, f32[64,1024]{1,0:T(8,128)}, u32[]{:S(2)}, u32[]{:S(2)}) collective-permute-start(f32[64,1024]{1,0:T(8,128)} %convert_select_fusion), channel_id=1, source_target_pairs={{0,1},{1,2},{2,3},{3,0},{4,5},{5,6},{6,7},{7,4},{8,9},{9,10},{10,1... | collective-permute-start | bytes 786440 | tf_op jit(solution)/shard_map/ppermute | solution.py:10
  180.6 32.9 %collective-permute-start = (f32[64]{0:T(128)S(1)}, f32[64]{0:T(128)}, u32[]{:S(2)}, u32[]{:S(2)}) collective-permute-start(f32[64]{0:T(128)S(1)} %get-tuple-element.206), channel_id=1, source_target_pairs={{0,1},{1,2},{2,3},{3,0},{4,5},{5,6},{6,7},{7,4},{8,9},{9,10},{10,1... | collective-permute-start | bytes 776 | tf_op jit(solution)/shard_map/ppermute | solution.py:10
  185.5 41.9 %collective-permute-start.12 = (f32[64,1024]{1,0:T(8,128)}, f32[64,1024]{1,0:T(8,128)}, u32[]{:S(2)}, u32[]{:S(2)}) collective-permute-start(f32[64,1024]{1,0:T(8,128)} %convolution_add_fusion), channel_id=1, source_target_pairs={{0,1},{1,2},{2,3},{3,0},{4,5},{5,6},{6,7},{7,4},{8,9},{9,10},{10,1... | collective-permute-start | bytes 786440 | tf_op jit(solution)/shard_map/ppermute | solution.py:10
  187.0 29.4 %collective-permute-start.4 = (f32[64]{0:T(128)}, f32[64]{0:T(128)}, u32[]{:S(2)}, u32[]{:S(2)}) collective-permute-start(f32[64]{0:T(128)} %get-tuple-element.205), channel_id=1, source_target_pairs={{0,1},{1,2},{2,3},{3,0},{4,5},{5,6},{6,7},{7,4},{8,9},{9,10},{10,1... | collective-permute-start | bytes 776 | tf_op jit(solution)/shard_map/ppermute | solution.py:10
  214.2 5.3 %collective-permute-start.1 = (f32[64]{0:T(128)S(1)}, f32[64]{0:T(128)S(1)}, u32[]{:S(2)}, u32[]{:S(2)}) collective-permute-start(f32[64]{0:T(128)S(1)} %max.43), channel_id=1, source_target_pairs={{0,1},{1,2},{2,3},{3,0},{4,5},{5,6},{6,7},{7,4},{8,9},{9,10},{10,1... | collective-permute-start | bytes 776 | tf_op jit(solution)/shard_map/ppermute | solution.py:10
  217.0 5.3 %collective-permute-start.5 = (f32[64]{0:T(128)S(1)}, f32[64]{0:T(128)S(1)}, u32[]{:S(2)}, u32[]{:S(2)}) collective-permute-start(f32[64]{0:T(128)S(1)} %get-tuple-element.172), channel_id=1, source_target_pairs={{0,1},{1,2},{2,3},{3,0},{4,5},{5,6},{6,7},{7,4},{8,9},{9,10},{10,1... | collective-permute-start | bytes 776 | tf_op jit(solution)/shard_map/ppermute | solution.py:10
  220.2 5.3 %collective-permute-start.2 = (f32[64]{0:T(128)S(1)}, f32[64]{0:T(128)S(1)}, u32[]{:S(2)}, u32[]{:S(2)}) collective-permute-start(f32[64]{0:T(128)S(1)} %max.44), channel_id=1, source_target_pairs={{0,1},{1,2},{2,3},{3,0},{4,5},{5,6},{6,7},{7,4},{8,9},{9,10},{10,1... | collective-permute-start | bytes 776 | tf_op jit(solution)/shard_map/ppermute | solution.py:10
  220.6 23.1 %slice-start = ((s8[8388608]{0:T(1024)(128)(4,1)}), s8[4194304]{0:T(1024)(128)(4,1)S(1)}, s32[]{:S(2)}) async-start(s8[8388608]{0:T(1024)(128)(4,1)} %bitcast.111), calls=%async_computation.1 | async-start | bytes 8388608
  222.4 23.1 %collective-permute-start.6 = (f32[64]{0:T(128)S(1)}, f32[64]{0:T(128)S(1)}, u32[]{:S(2)}, u32[]{:S(2)}) collective-permute-start(f32[64]{0:T(128)S(1)} %get-tuple-element.170), channel_id=1, source_target_pairs={{0,1},{1,2},{2,3},{3,0},{4,5},{5,6},{6,7},{7,4},{8,9},{9,10},{10,1... | collective-permute-start | bytes 776 | tf_op jit(solution)/shard_map/ppermute | solution.py:10
  227.1 10.0 %collective-permute-start.9 = (f32[64,1024]{1,0:T(8,128)S(1)}, f32[64,1024]{1,0:T(8,128)S(1)}, u32[]{:S(2)}, u32[]{:S(2)}) collective-permute-start(f32[64,1024]{1,0:T(8,128)S(1)} %select_add_fusion.2), channel_id=1, source_target_pairs={{0,1},{1,2},{2,3},{3,0},{4,5},{5,6},{6,7},{7,4},{8,9},{9,10},{10,1... | collective-permute-start | bytes 786440 | tf_op jit(solution)/shard_map/ppermute | solution.py:10
  227.5 16.3 %slice-start.1 = ((s8[8388608]{0:T(1024)(128)(4,1)}), s8[4194304]{0:T(1024)(128)(4,1)S(1)}, s32[]{:S(2)}) async-start(s8[8388608]{0:T(1024)(128)(4,1)} %bitcast.111), calls=%async_computation.2 | async-start | bytes 8388608
  232.6 11.1 %collective-permute-start.13 = (f32[64,1024]{1,0:T(8,128)S(1)}, f32[64,1024]{1,0:T(8,128)S(1)}, u32[]{:S(2)}, u32[]{:S(2)}) collective-permute-start(f32[64,1024]{1,0:T(8,128)S(1)} %multiply_add_fusion.2), channel_id=1, source_target_pairs={{0,1},{1,2},{2,3},{3,0},{4,5},{5,6},{6,7},{7,4},{8,9},{9,10},{10,1... | collective-permute-start | bytes 786440 | tf_op jit(solution)/shard_map/ppermute | solution.py:10
  237.2 11.4 %collective-permute-start.10 = (f32[64,1024]{1,0:T(8,128)S(1)}, f32[64,1024]{1,0:T(8,128)S(1)}, u32[]{:S(2)}, u32[]{:S(2)}) collective-permute-start(f32[64,1024]{1,0:T(8,128)S(1)} %select_add_fusion.1), channel_id=1, source_target_pairs={{0,1},{1,2},{2,3},{3,0},{4,5},{5,6},{6,7},{7,4},{8,9},{9,10},{10,1... | collective-permute-start | bytes 786440 | tf_op jit(solution)/shard_map/ppermute | solution.py:10
  245.4 9.8 %collective-permute-start.14 = (f32[64,1024]{1,0:T(8,128)S(1)}, f32[64,1024]{1,0:T(8,128)S(1)}, u32[]{:S(2)}, u32[]{:S(2)}) collective-permute-start(f32[64,1024]{1,0:T(8,128)S(1)} %multiply_add_fusion.1), channel_id=1, source_target_pairs={{0,1},{1,2},{2,3},{3,0},{4,5},{5,6},{6,7},{7,4},{8,9},{9,10},{10,1... | collective-permute-start | bytes 786440 | tf_op jit(solution)/shard_map/ppermute | solution.py:10
  248.7 16.5 %collective-permute-start.11 = (f32[64,1024]{1,0:T(8,128)S(1)}, f32[64,1024]{1,0:T(8,128)S(1)}, u32[]{:S(2)}, u32[]{:S(2)}) collective-permute-start(f32[64,1024]{1,0:T(8,128)S(1)} %select_add_fusion), channel_id=1, source_target_pairs={{0,1},{1,2},{2,3},{3,0},{4,5},{5,6},{6,7},{7,4},{8,9},{9,10},{10,1... | collective-permute-start | bytes 786440 | tf_op jit(solution)/shard_map/ppermute | solution.py:10
  255.2 10.0 %copy-start.3 = (bf16[64,1024]{1,0:T(8,128)(2,1)S(1)}, bf16[64,1024]{1,0:T(8,128)(2,1)}, u32[]{:S(2)}) copy-start(bf16[64,1024]{1,0:T(8,128)(2,1)} %param.20) | copy-start | bytes 393220
  256.9 8.3 %collective-permute-start.15 = (f32[64,1024]{1,0:T(8,128)S(1)}, f32[64,1024]{1,0:T(8,128)S(1)}, u32[]{:S(2)}, u32[]{:S(2)}) collective-permute-start(f32[64,1024]{1,0:T(8,128)S(1)} %multiply_add_fusion), channel_id=1, source_target_pairs={{0,1},{1,2},{2,3},{3,0},{4,5},{5,6},{6,7},{7,4},{8,9},{9,10},{10,1... | collective-permute-start | bytes 786440 | tf_op jit(solution)/shard_map/ppermute | solution.py:10
  257.0 8.2 %collective-permute-start.7 = (f32[64]{0:T(128)S(1)}, f32[64]{0:T(128)S(1)}, u32[]{:S(2)}, u32[]{:S(2)}) collective-permute-start(f32[64]{0:T(128)S(1)} %get-tuple-element.168), channel_id=1, source_target_pairs={{0,1},{1,2},{2,3},{3,0},{4,5},{5,6},{6,7},{7,4},{8,9},{9,10},{10,1... | collective-permute-start | bytes 776 | tf_op jit(solution)/shard_map/ppermute | solution.py:10
  257.2 8.9 %collective-permute-start.3 = (f32[64]{0:T(128)S(1)}, f32[64]{0:T(128)S(1)}, u32[]{:S(2)}, u32[]{:S(2)}) collective-permute-start(f32[64]{0:T(128)S(1)} %max.45), channel_id=1, source_target_pairs={{0,1},{1,2},{2,3},{3,0},{4,5},{5,6},{6,7},{7,4},{8,9},{9,10},{10,1... | collective-permute-start | bytes 776 | tf_op jit(solution)/shard_map/ppermute | solution.py:10
  (22 other events, 119.4 us)
Sparse Core Ops, SparseCore 0:
  109.2 57.0 all-gather.1
where the time goes:
time: 274 us; the launch traced here: 273 us
  matrix products  77.2 us (28%)
  local copies, waits for them, and re-layouts  74.1 us (27%)
  waiting for transfers between devices  60.3 us (22%)
  blocking collectives  25.8 us (9%)
  between operations  15.1 us (6%)
  starting transfers between devices  11.7 us (4%)
  other arithmetic  8.73 us (3%)
    ppermute x16, waiting for transfers between devices, shifted(): lax.ppermute(array, axis, [(i, (i + by) % count) for i in range(count)])  31.2 us
    all_gather x1, waiting for transfers between devices, per_device(): word_panel = lax.all_gather(embeds, 'vocab', axis=0, tiled=True)  29.1 us
    while x64, local copies, waits for them, and re-layouts  22.6 us
    gather x4, local copies, waits for them, and re-layouts, pick_targets(): jnp.take(word_panel, jnp.clip(row_spot, 0, count_words - 1), axis=0)  21 us
    dot_general x4, matrix products, char_features(): jnp.dot(windows.reshape(num_words * length, widths * embed_dim), masked,...  19.3 us
    slice x28, local copies, waits for them, and re-layouts, char_features(): padded[:, shift_at:shift_at + length, :]  17.8 us
    dot_general x4, matrix products, fold_panel(): lax.dot_general(row_block, word_panel, (((1,), (1,)), ((), ())), preferre...  17.4 us
    dot_general x4, matrix products, char_features(): jnp.dot(onehot.reshape(num_words * length, symbols), char_table, preferre...  16.7 us
  transfers between devices with their start and end apart: 17, of which 9 were waited for; matrix products, arithmetic and copies ran while one was open for 19% of the time, Pallas kernels for 0%

commit v1 on v0

--- a/solution.py
+++ b/solution.py
@@ -3,6 +3,28 @@
 import jax.numpy as jnp
 from jax import lax
 from jax.sharding import PartitionSpec as P
+
+
+def in_order(tiles, dim):
+    dims = list(tiles.shape[1:])
+    dims[dim] *= tiles.shape[0]
+    return jnp.moveaxis(tiles, 0, dim).reshape(dims)
+
+
+def collect(x, axis, dim):
+    size = lax.axis_size(axis)
+    pairs = [(i, (i + 1) % size) for i in range(size)]
+    back = [(b, a) for a, b in pairs]
+    lower, upper = ([], [])
+    for step in range(size - 1):
+        if step % 2 == 0:
+            lower.append(lax.ppermute(lower[-1] if lower else x, axis, pairs))
+        else:
+            upper.append(lax.ppermute(upper[-1] if upper else x, axis, back))
+    blocks = jnp.stack([*lower[::-1], x, *upper])
+    shift = lax.axis_index(axis) - len(lower)
+    blocks = blocks[(jnp.arange(size) - shift) % size]
+    return in_order(blocks, dim)
 
 
 def shifted(array, axis, by):
@@ -129,7 +151,7 @@
     blocks = lax.axis_size("blk")
     group_idx = lax.axis_index("blk")
     word_panel = lax.all_gather(embeds, "vocab", axis=0, tiled=True)
-    group_hidden = lax.all_gather(hidden, "blk", axis=0, tiled=True)
+    group_hidden = collect(hidden, "blk", 0)
     group_goal = lax.all_gather(targets, "blk", axis=0, tiled=True)
     owner_dev = group_goal // local_words
     in_group = owner_dev % blocks == group_idx

time: 274 us -> 274 us (level)
  blocking collectives: 25.8 us -> 8.23 us
  waiting for transfers between devices: 60.3 us -> 69.9 us
  starting transfers between devices: 11.7 us -> 18.5 us
    all_gather x1 -> x0, blocking collectives: 15.9 us -> none  [per_device(): group_hidden = lax.all_gather(hidden, 'blk', axis=0, tiled=True)]
    ppermute x0 -> x3, starting transfers between devices: none -> 7.35 us  [the longest x1 5.1 us: collect(): upper.append(lax.ppermute(upper[-1] if upper else x, axis, back))]
    ppermute x0 -> x3, waiting for transfers between devices: none -> 4.72 us  [the longest x2 4.72 us: collect(): lower.append(lax.ppermute(lower[-1] if lower else x, axis, pairs))]
    all_gather x1, waiting for transfers between devices: 29.1 us -> 33 us  [per_device(): word_panel = lax.all_gather(embeds, 'vocab', axis=0, tiled=True)]
  transfers between devices with their start and end apart: 17 -> 20, of which waited for: 9 -> 10; matrix products, arithmetic and copies ran while one was open for 19% -> 20% of each run, Pallas kernels for 0% -> 0%
where the time goes in v1:
time: 274 us; the launch traced here: 273 us
  matrix products  76.8 us (28%)
  local copies, waits for them, and re-layouts  74.6 us (27%)
  waiting for transfers between devices  69.9 us (26%)
  starting transfers between devices  18.5 us (7%)
  between operations  15 us (5%)
  other arithmetic  9.73 us (4%)
  blocking collectives  8.23 us (3%)
    all_gather x1, waiting for transfers between devices, per_device(): word_panel = lax.all_gather(embeds, 'vocab', axis=0, tiled=True)  33 us
    ppermute x16, waiting for transfers between devices, shifted(): lax.ppermute(array, axis, [(i, (i + by) % count) for i in range(count)])  32.1 us
    while x64, local copies, waits for them, and re-layouts  22.7 us
    gather x4, local copies, waits for them, and re-layouts, pick_targets(): jnp.take(word_panel, jnp.clip(row_spot, 0, count_words - 1), axis=0)  21 us
    dot_general x4, matrix products, char_features(): jnp.dot(windows.reshape(num_words * length, widths * embed_dim), masked,...  19.3 us
    slice x28, local copies, waits for them, and re-layouts, char_features(): padded[:, shift_at:shift_at + length, :]  17.9 us
    dot_general x4, matrix products, fold_panel(): lax.dot_general(row_block, word_panel, (((1,), (1,)), ((), ())), preferre...  17.1 us
    dot_general x4, matrix products, char_features(): jnp.dot(onehot.reshape(num_words * length, symbols), char_table, preferre...  16.7 us
  transfers between devices with their start and end apart: 20, of which 10 were waited for; matrix products, arithmetic and copies ran while one was open for 20% of the time, Pallas kernels for 0%

profile of v1, /device:TPU:0, one launch (start us, length us, event | category | flops | bytes accessed | tf_op | source)
XLA Modules:
  0.0 273.4 jit_solution(16857890084240592632)
XLA Ops:
  8.3 100.6 %while.13 = (s32[]{:T(128)}, bf16[4,128,1024]{2,1,0:T(8,128)(2,1)}, s32[4,128,50]{2,1,0:T(8,128)S(1)}, bf16[256,16]{0,1:T(8,128)(2,1)}, bf16[112,896]{1,0:T(8,12...) while((s32[]{:T(128)}, bf16[4,128,1024]{2,1,0:T(8,128)(2,1)}, ...), condition=%wide.region_2.3_spmd, body=%wide.region_0.2_spmd.sunk | while | flops 2662044928 | bytes 67010176 | solution.py:99
  8.5 4.2 %convolution_convert_fusion.4 = bf16[6400,16]{0,1:T(8,128)(2,1)S(1)} fusion(bf16[256,16]{0,1:T(8,128)(2,1)} %get-tuple-element.308, s32[6400]{0:T(1024)S(1)} %eq.55), kind=kOutput, calls=%fused_computation.6.clone.1 | convolution fusion | flops 54169600 | bytes 238592 | tf_op jit(solution)/shard_map/while/body/eval_jaxpr/dot_general | solution.py:45
  24.1 4.8 %select_reduce_fusion.2 = f32[128,896]{1,0:T(8,128)S(1)} fusion(pred[50,896]{1,0:T(8,128)(4,1)S(1)} %iota_compare_fusion.6, bf16[128,50,112]{0,2,1:T(8,128)(2,1)} %constant_dynamic-update-slice_fusion.20, bf16[112,896]{1,0:T(8,128)(2,1)S(1)} %copy-done.9, s32[896]{0:T(1024)S(1)} %fusion.152, s32[112]{0:T(128)S(1)} %and_select_fusion.7), kind=kOutput, calls=%fused_computation.5.clone.1 | convolution fusion | flops 1296060416 | bytes 2141888 | tf_op jit(solution)/shard_map/while/body/eval_jaxpr/dot_general | solution.py:56
  33.6 4.2 %convolution_convert_fusion.4 = bf16[6400,16]{0,1:T(8,128)(2,1)S(1)} fusion(bf16[256,16]{0,1:T(8,128)(2,1)} %get-tuple-element.308, s32[6400]{0:T(1024)S(1)} %eq.55), kind=kOutput, calls=%fused_computation.6.clone.1 | convolution fusion | flops 54169600 | bytes 238592 | tf_op jit(solution)/shard_map/while/body/eval_jaxpr/dot_general | solution.py:45
  49.3 4.8 %select_reduce_fusion.2 = f32[128,896]{1,0:T(8,128)S(1)} fusion(pred[50,896]{1,0:T(8,128)(4,1)S(1)} %iota_compare_fusion.6, bf16[128,50,112]{0,2,1:T(8,128)(2,1)} %constant_dynamic-update-slice_fusion.20, bf16[112,896]{1,0:T(8,128)(2,1)S(1)} %copy-done.9, s32[896]{0:T(1024)S(1)} %fusion.152, s32[112]{0:T(128)S(1)} %and_select_fusion.7), kind=kOutput, calls=%fused_computation.5.clone.1 | convolution fusion | flops 1296060416 | bytes 2141888 | tf_op jit(solution)/shard_map/while/body/eval_jaxpr/dot_general | solution.py:56
  58.8 4.2 %convolution_convert_fusion.4 = bf16[6400,16]{0,1:T(8,128)(2,1)S(1)} fusion(bf16[256,16]{0,1:T(8,128)(2,1)} %get-tuple-element.308, s32[6400]{0:T(1024)S(1)} %eq.55), kind=kOutput, calls=%fused_computation.6.clone.1 | convolution fusion | flops 54169600 | bytes 238592 | tf_op jit(solution)/shard_map/while/body/eval_jaxpr/dot_general | solution.py:45
  74.4 4.8 %select_reduce_fusion.2 = f32[128,896]{1,0:T(8,128)S(1)} fusion(pred[50,896]{1,0:T(8,128)(4,1)S(1)} %iota_compare_fusion.6, bf16[128,50,112]{0,2,1:T(8,128)(2,1)} %constant_dynamic-update-slice_fusion.20, bf16[112,896]{1,0:T(8,128)(2,1)S(1)} %copy-done.9, s32[896]{0:T(1024)S(1)} %fusion.152, s32[112]{0:T(128)S(1)} %and_select_fusion.7), kind=kOutput, calls=%fused_computation.5.clone.1 | convolution fusion | flops 1296060416 | bytes 2141888 | tf_op jit(solution)/shard_map/while/body/eval_jaxpr/dot_general | solution.py:56
  84.0 4.2 %convolution_convert_fusion.4 = bf16[6400,16]{0,1:T(8,128)(2,1)S(1)} fusion(bf16[256,16]{0,1:T(8,128)(2,1)} %get-tuple-element.308, s32[6400]{0:T(1024)S(1)} %eq.55), kind=kOutput, calls=%fused_computation.6.clone.1 | convolution fusion | flops 54169600 | bytes 238592 | tf_op jit(solution)/shard_map/while/body/eval_jaxpr/dot_general | solution.py:45
  99.6 4.8 %select_reduce_fusion.2 = f32[128,896]{1,0:T(8,128)S(1)} fusion(pred[50,896]{1,0:T(8,128)(4,1)S(1)} %iota_compare_fusion.6, bf16[128,50,112]{0,2,1:T(8,128)(2,1)} %constant_dynamic-update-slice_fusion.20, bf16[112,896]{1,0:T(8,128)(2,1)S(1)} %copy-done.9, s32[896]{0:T(1024)S(1)} %fusion.152, s32[112]{0:T(128)S(1)} %and_select_fusion.7), kind=kOutput, calls=%fused_computation.5.clone.1 | convolution fusion | flops 1296060416 | bytes 2141888 | tf_op jit(solution)/shard_map/while/body/eval_jaxpr/dot_general | solution.py:56
  108.9 5.1 %collective-permute-start.2 = (bf16[64,1024]{1,0:T(8,128)(2,1)}, bf16[64,1024]{1,0:T(8,128)(2,1)S(1)}, u32[]{:S(2)}, u32[]{:S(2)}) collective-permute-start(bf16[64,1024]{1,0:T(8,128)(2,1)} %param.20), channel_id=1, source_target_pairs={{1,0},{2,1},{3,2},{0,3},{5,4},{6,5},{7,6},{4,7},{9,8},{10,9},{11,1... | collective-permute-start | bytes 393224 | tf_op jit(solution)/shard_map/ppermute | solution.py:23
  115.6 8.2 %all-reduce.1 = s32[256]{0:T(256)S(1)} all-reduce(s32[256]{0:T(256)S(1)} %dynamic-update-slice), channel_id=1, replica_groups=mesh['vocab'=8,'blk'=4] {'blk'}, use_global_device_ids=true, to_apply=%add.1 | all-reduce | flops 256 | bytes 2048
  126.9 4.7 %collective-permute-done.1 = bf16[64,1024]{1,0:T(8,128)(2,1)S(1)} collective-permute-done((bf16[64,1024]{1,0:T(8,128)(2,1)S(1)}, bf16[64,1024]{1,0:T(8,128)(2,1)S(1)}, u32[]{:S(2)}, u32[]{:S(2)}) %collective-permute-start.1) | collective-permute-done | bytes 131104 | tf_op jit(solution)/shard_map/ppermute | solution.py:21
  133.1 33.0 %all-gather.2.cloned.1.call-done = bf16[4096,1024]{1,0:T(8,128)(2,1)} async-done(((bf16[512,1024]{1,0:T(8,128)(2,1)}), bf16[4096,1024]{1,0:T(8,128)(2,1)}) %all-gather.2.cloned.1.call-update) | async-done | bytes 8388624 | tf_op jit(solution)/shard_map/all_gather | solution.py:153
  166.2 5.3 %gather_fusion.1 = bf16[64,1024]{1,0:T(8,128)(2,1)S(1)} fusion(bf16[4096,1024]{1,0:T(8,128)(2,1)} %all-gather.2.cloned.1.call-done, s32[1024]{0:T(1024)S(1)} %pad_clamp_fusion.3), kind=kCustom, calls=%fused_computation.clone | custom fusion | bytes 262400 | tf_op jit(solution)/shard_map/jit(_take)/gather | solution.py:105
  173.7 6.3 %fusion.103 = (f32[64]{0:T(128)S(1)}, f32[64,4096]{1,0:T(8,128)S(1)}) fusion(bf16[4096,1024]{1,0:T(8,128)(2,1)} %all-gather.2.cloned.1.call-done, bf16[256,1024]{1,0:T(8,128)(2,1)S(1)} %bitcast.120, s32[]{:T(128)S(6)} %select_n.153), kind=kOutput, calls=%fused_computation.156 | convolution fusion | flops 537132992 | bytes 9568516 | tf_op jit(solution)/shard_map/dot_general | solution.py:113
  193.4 4.2 %fusion.106 = (f32[64]{0:T(128)}, f32[64,4096]{1,0:T(8,128)S(1)}) fusion(bf16[4096,1024]{1,0:T(8,128)(2,1)S(1)} %copy-done, bf16[256,1024]{1,0:T(8,128)(2,1)} %bitcast.123, s32[]{:T(128)S(6)} %select_n.159), kind=kOutput, calls=%fused_computation.159 | convolution fusion | flops 537132992 | bytes 9568516 | tf_op jit(solution)/shard_map/dot_general | solution.py:113
  197.6 5.3 %gather_fusion.2 = bf16[64,1024]{1,0:T(8,128)(2,1)S(1)} fusion(bf16[4096,1024]{1,0:T(8,128)(2,1)} %all-gather.2.cloned.1.call-done, s32[1024]{0:T(1024)S(1)} %pad_clamp_fusion.2), kind=kCustom, calls=%fused_computation.1.clone | custom fusion | bytes 262400 | tf_op jit(solution)/shard_map/jit(_take)/gather | solution.py:105
  202.8 5.3 %gather_fusion.3 = bf16[64,1024]{1,0:T(8,128)(2,1)S(1)} fusion(bf16[4096,1024]{1,0:T(8,128)(2,1)} %all-gather.2.cloned.1.call-done, s32[1024]{0:T(1024)S(1)} %pad_clamp_fusion.1), kind=kCustom, calls=%fused_computation.2.clone | custom fusion | bytes 262400 | tf_op jit(solution)/shard_map/jit(_take)/gather | solution.py:105
  208.1 5.3 %gather_fusion.4 = bf16[64,1024]{1,0:T(8,128)(2,1)S(1)} fusion(bf16[4096,1024]{1,0:T(8,128)(2,1)} %all-gather.2.cloned.1.call-done, s32[1024]{0:T(1024)S(1)} %pad_clamp_fusion), kind=kCustom, calls=%fused_computation.3.clone | custom fusion | bytes 262400 | tf_op jit(solution)/shard_map/jit(_take)/gather | solution.py:105
  227.3 5.2 %multiply_add_fusion.2 = f32[64,1024]{1,0:T(8,128)S(1)} fusion(f32[64,1024]{1,0:T(8,128)} %collective-permute-done.15, f32[64]{0:T(128)S(1)} %get-tuple-element.173, bf16[4096,1024]{1,0:T(8,128)(2,1)} %all-gather.2.cloned.1.call-done, f32[64,4096]{1,0:T(8,128)S(1)} %get-tuple-element.209, f32[64]{0:T(128)S(1)} %max.43), kind=kOutput, calls=%fused_computation.90 | convolution fusion | flops 537526272 | bytes 9961984 | tf_op jit(solution)/shard_map/dot_general | solution.py:120
  232.9 4.2 %collective-permute-done.12 = f32[64,1024]{1,0:T(8,128)S(1)} collective-permute-done((f32[64,1024]{1,0:T(8,128)S(1)}, f32[64,1024]{1,0:T(8,128)S(1)}, u32[]{:S(2)}, u32[]{:S(2)}) %collective-permute-start.12) | collective-permute-done | bytes 262176 | tf_op jit(solution)/shard_map/ppermute | solution.py:32
  237.3 6.3 %collective-permute-done.16 = f32[64,1024]{1,0:T(8,128)S(1)} collective-permute-done((f32[64,1024]{1,0:T(8,128)S(1)}, f32[64,1024]{1,0:T(8,128)S(1)}, u32[]{:S(2)}, u32[]{:S(2)}) %collective-permute-start.16) | collective-permute-done | bytes 262176 | tf_op jit(solution)/shard_map/ppermute | solution.py:32
  248.7 6.4 %collective-permute-done.17 = f32[64,1024]{1,0:T(8,128)S(1)} collective-permute-done((f32[64,1024]{1,0:T(8,128)S(1)}, f32[64,1024]{1,0:T(8,128)S(1)}, u32[]{:S(2)}, u32[]{:S(2)}) %collective-permute-start.17) | collective-permute-done | bytes 262176 | tf_op jit(solution)/shard_map/ppermute | solution.py:32
  259.4 5.7 %collective-permute-done.10 = f32[64]{0:T(128)S(1)} collective-permute-done((f32[64]{0:T(128)S(1)}, f32[64]{0:T(128)S(1)}, u32[]{:S(2)}, u32[]{:S(2)}) %collective-permute-start.10) | collective-permute-done | bytes 288 | tf_op jit(solution)/shard_map/ppermute | solution.py:32
  (242 shorter events, 111.3 us)
Async XLA Ops:
  7.2 159.0 %all-gather.2.cloned.1.call-start = ((), (), s32[]{:S(2)}) async-start(), calls=%async_computation | async-start | bytes 9437184 | tf_op jit(solution)/shard_map/all_gather | solution.py:153
  8.2 105.8 %copy-start.11 = (u32[32]{0:T(128)S(1)}, u32[32]{0:T(128)}, u32[]{:S(2)}) copy-start(u32[32]{0:T(128)} %constant.234) | copy-start | bytes 388
  8.3 107.1 %copy-start.10 = (s32[64]{0:T(128)S(1)}, s32[64]{0:T(128)}, u32[]{:S(2)}) copy-start(s32[64]{0:T(128)} %param.21) | copy-start | bytes 772
  108.9 17.9 %collective-permute-start.2 = (bf16[64,1024]{1,0:T(8,128)(2,1)}, bf16[64,1024]{1,0:T(8,128)(2,1)S(1)}, u32[]{:S(2)}, u32[]{:S(2)}) collective-permute-start(bf16[64,1024]{1,0:T(8,128)(2,1)} %param.20), channel_id=1, source_target_pairs={{1,0},{2,1},{3,2},{0,3},{5,4},{6,5},{7,6},{4,7},{9,8},{10,9},{11,1... | collective-permute-start | bytes 393224 | tf_op jit(solution)/shard_map/ppermute | solution.py:23
  114.0 10.5 %collective-permute-start = (bf16[64,1024]{1,0:T(8,128)(2,1)}, bf16[64,1024]{1,0:T(8,128)(2,1)S(1)}, u32[]{:S(2)}, u32[]{:S(2)}) collective-permute-start(bf16[64,1024]{1,0:T(8,128)(2,1)} %param.20), channel_id=1, source_target_pairs={{0,1},{1,2},{2,3},{3,0},{4,5},{5,6},{6,7},{7,4},{8,9},{9,10},{10,1... | collective-permute-start | bytes 393224 | tf_op jit(solution)/shard_map/ppermute | solution.py:21
  124.6 7.0 %collective-permute-start.1 = (bf16[64,1024]{1,0:T(8,128)(2,1)S(1)}, bf16[64,1024]{1,0:T(8,128)(2,1)S(1)}, u32[]{:S(2)}, u32[]{:S(2)}) collective-permute-start(bf16[64,1024]{1,0:T(8,128)(2,1)S(1)} %collective-permute-done), channel_id=1, source_target_pairs={{0,1},{1,2},{2,3},{3,0},{4,5},{5,6},{6,7},{7,4},{8,9},{9,10},{10,1... | collective-permute-start | bytes 393224 | tf_op jit(solution)/shard_map/ppermute | solution.py:21
  133.1 56.9 %copy-start.2 = (bf16[4,64,1024]{2,1,0:T(8,128)(2,1)}, bf16[4,64,1024]{2,1,0:T(8,128)(2,1)S(1)}, u32[]{:S(2)}) copy-start(bf16[4,64,1024]{2,1,0:T(8,128)(2,1)S(1)} %gather_fusion) | copy-start | bytes 1572868
  172.3 53.7 %collective-permute-start.11 = (f32[64,1024]{1,0:T(8,128)}, f32[64,1024]{1,0:T(8,128)}, u32[]{:S(2)}, u32[]{:S(2)}) collective-permute-start(f32[64,1024]{1,0:T(8,128)} %convert_select_fusion), channel_id=1, source_target_pairs={{0,1},{1,2},{2,3},{3,0},{4,5},{5,6},{6,7},{7,4},{8,9},{9,10},{10,1... | collective-permute-start | bytes 786440 | tf_op jit(solution)/shard_map/ppermute | solution.py:32
  180.0 33.3 %collective-permute-start.3 = (f32[64]{0:T(128)S(1)}, f32[64]{0:T(128)}, u32[]{:S(2)}, u32[]{:S(2)}) collective-permute-start(f32[64]{0:T(128)S(1)} %get-tuple-element.206), channel_id=1, source_target_pairs={{0,1},{1,2},{2,3},{3,0},{4,5},{5,6},{6,7},{7,4},{8,9},{9,10},{10,1... | collective-permute-start | bytes 776 | tf_op jit(solution)/shard_map/ppermute | solution.py:32
  184.8 42.5 %collective-permute-start.15 = (f32[64,1024]{1,0:T(8,128)}, f32[64,1024]{1,0:T(8,128)}, u32[]{:S(2)}, u32[]{:S(2)}) collective-permute-start(f32[64,1024]{1,0:T(8,128)} %convolution_add_fusion), channel_id=1, source_target_pairs={{0,1},{1,2},{2,3},{3,0},{4,5},{5,6},{6,7},{7,4},{8,9},{9,10},{10,1... | collective-permute-start | bytes 786440 | tf_op jit(solution)/shard_map/ppermute | solution.py:32
  186.3 29.5 %collective-permute-start.7 = (f32[64]{0:T(128)}, f32[64]{0:T(128)}, u32[]{:S(2)}, u32[]{:S(2)}) collective-permute-start(f32[64]{0:T(128)} %get-tuple-element.205), channel_id=1, source_target_pairs={{0,1},{1,2},{2,3},{3,0},{4,5},{5,6},{6,7},{7,4},{8,9},{9,10},{10,1... | collective-permute-start | bytes 776 | tf_op jit(solution)/shard_map/ppermute | solution.py:32
  214.0 5.3 %collective-permute-start.4 = (f32[64]{0:T(128)S(1)}, f32[64]{0:T(128)S(1)}, u32[]{:S(2)}, u32[]{:S(2)}) collective-permute-start(f32[64]{0:T(128)S(1)} %max.43), channel_id=1, source_target_pairs={{0,1},{1,2},{2,3},{3,0},{4,5},{5,6},{6,7},{7,4},{8,9},{9,10},{10,1... | collective-permute-start | bytes 776 | tf_op jit(solution)/shard_map/ppermute | solution.py:32
  216.4 5.3 %collective-permute-start.8 = (f32[64]{0:T(128)S(1)}, f32[64]{0:T(128)S(1)}, u32[]{:S(2)}, u32[]{:S(2)}) collective-permute-start(f32[64]{0:T(128)S(1)} %get-tuple-element.172), channel_id=1, source_target_pairs={{0,1},{1,2},{2,3},{3,0},{4,5},{5,6},{6,7},{7,4},{8,9},{9,10},{10,1... | collective-permute-start | bytes 776 | tf_op jit(solution)/shard_map/ppermute | solution.py:32
  220.0 5.3 %collective-permute-start.5 = (f32[64]{0:T(128)S(1)}, f32[64]{0:T(128)S(1)}, u32[]{:S(2)}, u32[]{:S(2)}) collective-permute-start(f32[64]{0:T(128)S(1)} %max.44), channel_id=1, source_target_pairs={{0,1},{1,2},{2,3},{3,0},{4,5},{5,6},{6,7},{7,4},{8,9},{9,10},{10,1... | collective-permute-start | bytes 776 | tf_op jit(solution)/shard_map/ppermute | solution.py:32
  220.1 23.5 %slice-start = ((s8[8388608]{0:T(1024)(128)(4,1)}), s8[4194304]{0:T(1024)(128)(4,1)S(1)}, s32[]{:S(2)}) async-start(s8[8388608]{0:T(1024)(128)(4,1)} %bitcast.118), calls=%async_computation.1 | async-start | bytes 8388608
  221.8 23.6 %collective-permute-start.9 = (f32[64]{0:T(128)S(1)}, f32[64]{0:T(128)S(1)}, u32[]{:S(2)}, u32[]{:S(2)}) collective-permute-start(f32[64]{0:T(128)S(1)} %get-tuple-element.170), channel_id=1, source_target_pairs={{0,1},{1,2},{2,3},{3,0},{4,5},{5,6},{6,7},{7,4},{8,9},{9,10},{10,1... | collective-permute-start | bytes 776 | tf_op jit(solution)/shard_map/ppermute | solution.py:32
  227.0 10.1 %collective-permute-start.12 = (f32[64,1024]{1,0:T(8,128)S(1)}, f32[64,1024]{1,0:T(8,128)S(1)}, u32[]{:S(2)}, u32[]{:S(2)}) collective-permute-start(f32[64,1024]{1,0:T(8,128)S(1)} %select_add_fusion.2), channel_id=1, source_target_pairs={{0,1},{1,2},{2,3},{3,0},{4,5},{5,6},{6,7},{7,4},{8,9},{9,10},{10,1... | collective-permute-start | bytes 786440 | tf_op jit(solution)/shard_map/ppermute | solution.py:32
  232.5 11.1 %collective-permute-start.16 = (f32[64,1024]{1,0:T(8,128)S(1)}, f32[64,1024]{1,0:T(8,128)S(1)}, u32[]{:S(2)}, u32[]{:S(2)}) collective-permute-start(f32[64,1024]{1,0:T(8,128)S(1)} %multiply_add_fusion.2), channel_id=1, source_target_pairs={{0,1},{1,2},{2,3},{3,0},{4,5},{5,6},{6,7},{7,4},{8,9},{9,10},{10,1... | collective-permute-start | bytes 786440 | tf_op jit(solution)/shard_map/ppermute | solution.py:32
  237.2 11.3 %collective-permute-start.13 = (f32[64,1024]{1,0:T(8,128)S(1)}, f32[64,1024]{1,0:T(8,128)S(1)}, u32[]{:S(2)}, u32[]{:S(2)}) collective-permute-start(f32[64,1024]{1,0:T(8,128)S(1)} %select_add_fusion.1), channel_id=1, source_target_pairs={{0,1},{1,2},{2,3},{3,0},{4,5},{5,6},{6,7},{7,4},{8,9},{9,10},{10,1... | collective-permute-start | bytes 786440 | tf_op jit(solution)/shard_map/ppermute | solution.py:32
  245.3 9.8 %collective-permute-start.17 = (f32[64,1024]{1,0:T(8,128)S(1)}, f32[64,1024]{1,0:T(8,128)S(1)}, u32[]{:S(2)}, u32[]{:S(2)}) collective-permute-start(f32[64,1024]{1,0:T(8,128)S(1)} %multiply_add_fusion.1), channel_id=1, source_target_pairs={{0,1},{1,2},{2,3},{3,0},{4,5},{5,6},{6,7},{7,4},{8,9},{9,10},{10,1... | collective-permute-start | bytes 786440 | tf_op jit(solution)/shard_map/ppermute | solution.py:32
  248.6 16.5 %collective-permute-start.14 = (f32[64,1024]{1,0:T(8,128)S(1)}, f32[64,1024]{1,0:T(8,128)S(1)}, u32[]{:S(2)}, u32[]{:S(2)}) collective-permute-start(f32[64,1024]{1,0:T(8,128)S(1)} %select_add_fusion), channel_id=1, source_target_pairs={{0,1},{1,2},{2,3},{3,0},{4,5},{5,6},{6,7},{7,4},{8,9},{9,10},{10,1... | collective-permute-start | bytes 786440 | tf_op jit(solution)/shard_map/ppermute | solution.py:32
  256.8 8.3 %collective-permute-start.18 = (f32[64,1024]{1,0:T(8,128)S(1)}, f32[64,1024]{1,0:T(8,128)S(1)}, u32[]{:S(2)}, u32[]{:S(2)}) collective-permute-start(f32[64,1024]{1,0:T(8,128)S(1)} %multiply_add_fusion), channel_id=1, source_target_pairs={{0,1},{1,2},{2,3},{3,0},{4,5},{5,6},{6,7},{7,4},{8,9},{9,10},{10,1... | collective-permute-start | bytes 786440 | tf_op jit(solution)/shard_map/ppermute | solution.py:32
  256.9 8.2 %collective-permute-start.10 = (f32[64]{0:T(128)S(1)}, f32[64]{0:T(128)S(1)}, u32[]{:S(2)}, u32[]{:S(2)}) collective-permute-start(f32[64]{0:T(128)S(1)} %get-tuple-element.168), channel_id=1, source_target_pairs={{0,1},{1,2},{2,3},{3,0},{4,5},{5,6},{6,7},{7,4},{8,9},{9,10},{10,1... | collective-permute-start | bytes 776 | tf_op jit(solution)/shard_map/ppermute | solution.py:32
  257.0 9.0 %collective-permute-start.6 = (f32[64]{0:T(128)S(1)}, f32[64]{0:T(128)S(1)}, u32[]{:S(2)}, u32[]{:S(2)}) collective-permute-start(f32[64]{0:T(128)S(1)} %max.45), channel_id=1, source_target_pairs={{0,1},{1,2},{2,3},{3,0},{4,5},{5,6},{6,7},{7,4},{8,9},{9,10},{10,1... | collective-permute-start | bytes 776 | tf_op jit(solution)/shard_map/ppermute | solution.py:32
  (25 other events, 154.5 us)
Sparse Core Ops, SparseCore 0:
  109.1 57.0 all-gather.1
